TPU v7x, 512 devices: a whole 4x8x8 slice. The times are simulated.
512 devices in a mesh: row: 16 (over y_lo, x, core), col: 8 (over z), seq: 4 (over y_hi).
Axes of the slice: x: 4, y: 8 (y_hi: 4, y_lo: 2; y = y_hi * 2 + y_lo), z: 8, core: 2. Of those that a mesh axis runs over, the one named last changes fastest.
Arguments:
- left_piece: bfloat16 [512, 32, 1024], P('seq', None, 'row'), may hold values from -6 to 6
- right_piece: bfloat16 [512, 32, 1024], P('seq', 'row', 'col'), may hold values from -6 to 6
- proj_weight: bfloat16 [1024, 128], replicated, may hold values from -4 to 4
- proj_bias: float32 [128], replicated, may hold values from -3 to 3
- pair_rep: bfloat16 [1024, 1024, 128], P(('row', 'seq'), 'col'), may hold values from -6 to 6
- norm_gain: float32 [128], replicated, may hold values from 0.5 to 1.5
- up_weight: bfloat16 [128, 512], replicated, may hold values from -0.5 to 0.5
- up_bias: float32 [512], replicated, may hold values from -3 to 3
- down_weight: bfloat16 [512, 128], replicated, may hold values from -0.25 to 0.25
- down_bias: float32 [128], replicated, may hold values from -3 to 3
Outputs:
- refined: bfloat16 [1024, 1024, 128], P(('row', 'seq'), 'col')
All inputs are finite; a program needn't handle non-finite values.
Results may differ from a plain program's by a relative error of at most 0.0085.
Values may be sent and summed in bfloat16 or wider, within the bound.
A program may use at most 64 MiB of HBM per device.

v0:
```python
import jax
import jax.numpy as jnp
from jax import lax
from jax.sharding import PartitionSpec as P

epsilon = 1e-05


def project_block(row_slab, right_all, proj_weight):
    seq_count, channels, row_count = row_slab.shape
    columns = right_all.shape[2]
    left_mat = row_slab.reshape(seq_count, channels * row_count)
    right_mat = right_all.reshape(seq_count, channels * columns)
    outer_prod = lax.dot_general(
        left_mat, right_mat, (((0,), (0,)), ((), ())), preferred_element_type=jnp.float32
    ).astype(jnp.bfloat16)
    outer_prod = outer_prod.reshape(channels, row_count, channels, columns).transpose(1, 3, 0, 2)
    outer_prod = outer_prod.reshape(row_count * columns, channels * channels)
    result = jnp.dot(outer_prod, proj_weight, preferred_element_type=jnp.float32)
    return result.reshape(row_count, columns, proj_weight.shape[1])


def project_rows(row_slab, right_all, proj_weight):
    seq_count, channels, row_count = row_slab.shape
    sub_rows = 8
    pieces = row_slab.reshape(seq_count, channels, row_count // sub_rows, sub_rows)
    pieces = jnp.moveaxis(pieces, 2, 0)
    result = lax.map(lambda portion: project_block(portion, right_all, proj_weight), pieces)
    return result.reshape(row_count, right_all.shape[2], proj_weight.shape[1])


def transition(middle, norm_gain, up_weight, up_bias, down_weight, down_bias):
    row_count, columns, channels = middle.shape
    values = middle.astype(jnp.float32).reshape(row_count * columns, channels)
    center = jnp.mean(values, axis=1, keepdims=True)
    spread = jnp.mean(jnp.square(values - center), axis=1, keepdims=True)
    normed = ((values - center) * lax.rsqrt(spread + epsilon) * norm_gain).astype(jnp.bfloat16)
    hidden = jnp.maximum(
        jnp.dot(normed, up_weight, preferred_element_type=jnp.float32) + up_bias, 0.0
    ).astype(jnp.bfloat16)
    result = values + jnp.dot(hidden, down_weight, preferred_element_type=jnp.float32) + down_bias
    return result.astype(jnp.bfloat16).reshape(row_count, columns, channels)


def gather_right(right_part):
    return lax.all_gather(right_part, "row", axis=1, tiled=True)


def move_cols(tile):
    return lax.all_to_all(tile, "col", split_axis=0, concat_axis=2, tiled=True)


def on_device(
    left_piece,
    right_piece,
    proj_weight,
    proj_bias,
    pair_rep,
    norm_gain,
    up_weight,
    up_bias,
    down_weight,
    down_bias,
):
    own_rows = pair_rep.shape[0]
    columns = pair_rep.shape[1]
    channels = pair_rep.shape[2]
    groups = lax.axis_size("seq")
    seq_index = lax.axis_index("seq")
    group_len = left_piece.shape[0]
    seq_total = group_len * groups
    left_all, right_seq = (
        lax.all_gather(left_piece, "seq", axis=0, tiled=True),
        lax.all_gather(right_piece, "seq", axis=0, tiled=True),
    )
    right_all = gather_right(right_seq)
    offset = seq_index * own_rows
    summed = jnp.zeros((own_rows, columns, channels), jnp.float32)
    for group_id in range(groups):
        left_group = left_all[group_id * group_len : (group_id + 1) * group_len]
        row_slab = lax.dynamic_slice_in_dim(left_group, offset, own_rows, 2)
        right_group = right_all[group_id * group_len : (group_id + 1) * group_len]
        summed = summed + project_rows(row_slab, right_group, proj_weight)
    update = (summed / seq_total + proj_bias).astype(jnp.bfloat16)
    col_count = lax.axis_size("col")
    rowseq_count = lax.axis_size(("row", "seq"))
    run_len = own_rows // col_count
    section_one = move_cols(update.reshape(col_count, run_len, columns, channels))
    section_two = lax.all_to_all(
        section_one.reshape(run_len, rowseq_count, own_rows, channels),
        ("row", "seq"),
        split_axis=1,
        concat_axis=0,
        tiled=True,
    )
    section_three = move_cols(
        section_two.reshape(col_count, rowseq_count // col_count, 1, run_len, own_rows, channels)
    )
    mirrored = section_three.reshape(columns, own_rows, channels).transpose(1, 0, 2)
    middle = (
        pair_rep.astype(jnp.float32)
        + 0.5 * (update.astype(jnp.float32) + mirrored.astype(jnp.float32))
    ).astype(jnp.bfloat16)
    return transition(middle, norm_gain, up_weight, up_bias, down_weight, down_bias)


def solution(mesh):
    in_specs = (
        P("seq", None, "row"),
        P("seq", "row", "col"),
        P(),
        P(),
        P(("row", "seq"), "col", None),
        P(),
        P(),
        P(),
        P(),
        P(),
    )
    out_specs = P(("row", "seq"), "col", None)
    return jax.shard_map(
        on_device, mesh=mesh, in_specs=in_specs, out_specs=out_specs, check_vma=False
    )
```

profile of v0, /device:TPU:1, one launch (start us, length us, event | category | flops | bytes accessed | tf_op | source)
XLA Modules:
  0.0 234.8 jit_solution(6227691487281684803)
XLA Ops:
  7.3 15.7 %all_gather.10 = bf16[512,2,128]{2,1,0:T(2,128)(2,1)S(1)} all-gather(bf16[128,2,128]{2,1,0:T(2,128)(2,1)} %param.19), channel_id=1, replica_groups=mesh['row'=16,'col'=8,'seq'=4] {'seq'}, dimensions={0}, use_global_device_ids=true | all-gather | bytes 327680 | tf_op jit(solution)/shard_map/all_gather | solution.py:74
  23.8 43.0 %all-gather.3.cloned.1.call-done = bf16[512,32,64]{0,2,1:T(8,128)(2,1)} async-done(((bf16[128,32,64]{0,2,1:T(8,128)(2,1)}), bf16[512,32,64]{0,2,1:T(8,128)(2,1)}) %all-gather.3.cloned.1.call-update) | async-done | bytes 2097168 | tf_op jit(solution)/shard_map/all_gather | solution.py:73
  66.7 1.8 fusion.68
  69.9 46.1 %all-gather.5.cloned.1.call-done = bf16[512,32,128]{2,0,1:T(8,128)(2,1)} async-done(((bf16[512,2,128]{2,0,1:T(8,128)(2,1)}), bf16[512,32,128]{2,0,1:T(8,128)(2,1)}) %all-gather.5.cloned.1.call-update) | async-done | bytes 4194320 | tf_op jit(solution)/shard_map/all_gather | solution.py:46
  116.0 2.8 %fusion.67 = (bf16[128,32,128]{2,0,1:T(8,128)(2,1)S(1)}, bf16[128,32,128]{2,0,1:T(8,128)(2,1)S(1)}, bf16[128,32,128]{2,0,1:T(8,128)(2,1)S(1)}, bf16[128,32,128]{2,0,1:T(8,128)(2,1)S(1)}) fusion(bf16[512,32,128]{2,0,1:T(8,128)(2,1)} %all-gather.5.cloned.1.call-done), kind=kLoop, calls=%fused_computation.71 | loop fusion | bytes 8388608 | tf_op jit(solution)/shard_map/slice | solution.py:82
  120.9 1.7 copy.102
  122.6 1.1 broadcast.42.clone.2
  123.7 7.8 %while.40 = (s32[]{:T(128)}, f32[2,8,128,128]{3,2,1,0:T(8,128)}, bf16[2,128,32,8]{1,3,0,2:T(8,128)(2,1)}, bf16[128,32,128]{2,1,0:T(8,128)(2,1)}, bf16[1024,128]{1,0:T(8,128)(2,1)}, /*index=5*/s32[]{:T(128)}) while((s32[]{:T(128)}, f32[2,8,128,128]{3,2,1,0:T(8,128)}, bf16[2,128,32,8]{1,3,0,2:T(8,128)(2,1)}, bf16[128,32,128]{2,1,0:T(8,128)(2,1)}, ...), condition=%wide.region_1.2_spmd, body=%wide.region_0.1_spmd.sunk | while | flops 537919488 | bytes 15532201 | solution.py:28
  123.7 2.1 convolution_convert_fusion.8
  125.8 0.8 fusion.96
  126.6 1.0 copy-done.2
  127.6 2.1 convolution_convert_fusion.8
  129.7 0.8 fusion.96
  130.5 1.0 copy-done.2
  131.5 1.1 broadcast.42.clone.1
  132.5 6.9 %while.42 = (s32[]{:T(128)}, f32[2,8,128,128]{3,2,1,0:T(8,128)}, bf16[2,128,32,8]{1,3,0,2:T(8,128)(2,1)}, bf16[128,32,128]{2,1,0:T(8,128)(2,1)S(1)}, bf16[1024,128]{1,0:T(8,128)(2,1)}, /*index=5*/s32[]{:T(128)}) while((s32[]{:T(128)}, f32[2,8,128,128]{3,2,1,0:T(8,128)}, bf16[2,128,32,8]{1,3,0,2:T(8,128)(2,1)}, ...), condition=%wide.region_5.6_spmd, body=%wide.region_4.5_spmd.sunk | while | flops 537919488 | bytes 15532201 | solution.py:28
  132.5 1.7 convolution_convert_fusion.10
  134.2 0.8 fusion.106
  135.0 1.0 copy-done.5
  136.0 1.7 convolution_convert_fusion.10
  137.7 0.8 fusion.106
  138.5 1.0 copy-done.5
  139.6 3.5 %while.43 = (s32[]{:T(128)}, f32[2,8,128,128]{3,2,1,0:T(8,128)S(1)}, bf16[2,128,32,8]{1,3,0,2:T(8,128)(2,1)S(1)}, bf16[128,32,128]{2,1,0:T(8,128)(2,1)S(1)}, bf16[1024,128]{1,0:T(8,128)(2,1)}, /*index=5*/s32[]{:T(128)}) while((s32[]{:T(128)}, f32[2,8,128,128]{3,2,1,0:T(8,128)S(1)}, bf16[2,128,32,8]{1,3,0,2:T(8,128)(2,1)S(1)}, ...), condition=%wide.region_7.8_spmd, body=%wide.region_6.7_spmd.sunk | while | flops 537919488 | bytes 7143537 | solution.py:28
  143.2 0.9 copy-done.6
  144.1 3.6 %while.41 = (s32[]{:T(128)}, f32[2,8,128,128]{3,2,1,0:T(8,128)S(1)}, bf16[2,128,32,8]{1,3,0,2:T(8,128)(2,1)S(1)}, bf16[128,32,128]{2,1,0:T(8,128)(2,1)S(1)}, bf16[1024,128]{1,0:T(8,128)(2,1)}, /*index=5*/s32[]{:T(128)}) while((s32[]{:T(128)}, f32[2,8,128,128]{3,2,1,0:T(8,128)S(1)}, bf16[2,128,32,8]{1,3,0,2:T(8,128)(2,1)S(1)}, ...), condition=%wide.region_3.4_spmd, body=%wide.region_2.3_spmd.sunk | while | flops 537919488 | bytes 7143537 | solution.py:28
  145.1 0.8 fusion.101
  147.7 1.8 add_multiply_fusion
  149.7 24.2 %all_to_all.39 = bf16[8,2,128,128]{3,2,1,0:T(8,128)(2,1)S(1)} all-to-all(bf16[8,2,128,128]{3,2,1,0:T(8,128)(2,1)S(1)} %add_convert_fusion), channel_id=1, replica_groups=mesh['row'=16,'col'=8,'seq'=4] {'col'}, dimensions={0} | all-to-all | bytes 1048576 | tf_op jit(solution)/shard_map/all_to_all | solution.py:50
  174.0 28.1 %all_to_all.40 = bf16[2,64,16,128]{3,2,0,1:T(8,128)(2,1)S(1)} all-to-all(bf16[2,64,16,128]{3,2,0,1:T(8,128)(2,1)S(1)} %copy.111), channel_id=1, replica_groups=mesh['row'=16,'col'=8,'seq'=4] {'row','seq'}, dimensions={1} | all-to-all | bytes 1048576 | tf_op jit(solution)/shard_map/all_to_all | solution.py:89
  202.1 20.6 %all_to_all.41 = bf16[8,8,1,2,16,128]{5,4,3,1,2,0:T(8,128)(2,1)S(1)} all-to-all(bf16[8,8,1,2,16,128]{5,4,3,1,2,0:T(8,128)(2,1)S(1)} %bitcast.205), channel_id=1, replica_groups=mesh['row'=16,'col'=8,'seq'=4] {'col'}, dimensions={0} | all-to-all | bytes 1048576 | tf_op jit(solution)/shard_map/all_to_all | solution.py:50
  222.8 1.0 fusion.60
  225.9 2.0 fusion.57
  (77 shorter events, 13.7 us)
Async XLA Ops:
  6.5 219.3 %copy-start = (bf16[512,128]{1,0:T(8,128)(2,1)S(1)}, bf16[512,128]{1,0:T(8,128)(2,1)}, u32[]{:S(2)}) copy-start(bf16[512,128]{1,0:T(8,128)(2,1)} %param.26) | copy-start | bytes 393220
  6.5 60.2 %all-gather.3.cloned.1.call-start = ((), (), s32[]{:S(2)}) async-start(), calls=%async_computation.3 | async-start | bytes 2621440 | tf_op jit(solution)/shard_map/all_gather | solution.py:73
  7.3 108.8 %all-gather.5.cloned.1.call-start = ((), (), s32[]{:S(2)}) async-start(), calls=%async_computation.4 | async-start | bytes 4456448 | tf_op jit(solution)/shard_map/all_gather | solution.py:46
  123.7 2.1 copy-start.1
  123.7 2.1 copy-start.10
  126.6 1.0 copy-start.2
  127.6 2.1 copy-start.1
  127.6 2.1 copy-start.10
  130.5 1.0 copy-start.2
  132.5 1.7 copy-start.4
  132.5 1.7 copy-start.11
  135.0 1.0 copy-start.5
  136.0 1.7 copy-start.4
  136.0 1.7 copy-start.11
  138.5 1.0 copy-start.5
  139.6 1.0 copy-start.12
  141.3 1.0 copy-start.12
  143.1 1.0 copy-start.6
  144.1 3.6 %copy-start.3 = (f32[2,8,128,128]{3,2,1,0:T(8,128)S(1)}, f32[2,8,128,128]{3,2,1,0:T(8,128)}, u32[]{:S(2)}) copy-start(f32[2,8,128,128]{3,2,1,0:T(8,128)} %get-tuple-element.113) | copy-start | bytes 3145732
  144.1 1.0 copy-start.13
  145.9 1.0 copy-start.13
  147.7 1.9 copy-start.8
  174.0 48.8 %copy-start.7 = (bf16[16,128,128]{2,1,0:T(8,128)(2,1)S(1)}, bf16[16,128,128]{2,1,0:T(8,128)(2,1)}, u32[]{:S(2)}) copy-start(bf16[16,128,128]{2,1,0:T(8,128)(2,1)} %param.22) | copy-start | bytes 1572868
  223.8 1.4 copy-start.9
  224.2 1.7 copy-start.14
  224.2 1.7 copy-start.15
  224.2 1.7 copy-start.16
Sparse Core Ops, SparseCore 0:
  9.4 57.2 all-gather.2
  68.9 47.1 all-gather.4
where the time goes:
time: 235 us
  waiting for transfers between devices  89.8 us (38%)
  blocking collectives  88.6 us (38%)
  local copies, waits for them, and re-layouts  18.9 us (8%)
  matrix products  18.8 us (8%)
  between operations  13.7 us (6%)
  other arithmetic  4.69 us (2%)
    all_gather x1, waiting for transfers between devices, gather_right(): return lax.all_gather(right_part, 'row', axis=1, tiled=True)  46.1 us
    all_to_all x2, blocking collectives, move_cols(): return lax.all_to_all(tile, 'col', split_axis=0, concat_axis=2, tiled=True)  44.8 us
    all_gather x1, waiting for transfers between devices, on_device(): lax.all_gather(left_piece, 'seq', axis=0, tiled=True)  43 us
    all_to_all x1, blocking collectives, on_device(): lax.all_to_all(section_one.reshape(run_len, rowseq_count, own_rows, chann...  28.1 us
    all_gather x1, blocking collectives, on_device(): lax.all_gather(right_piece, 'seq', axis=0, tiled=True)  15.7 us
    dot_general x8, matrix products, project_block(): lax.dot_general(left_mat, right_mat, (((0,), (0,)), ((), ())), preferred_...  10.5 us
    dot_general x8, matrix products, project_block(): jnp.dot(outer_prod, proj_weight, preferred_element_type=jnp.float32)  6.24 us
    while x32, local copies, waits for them, and re-layouts  4.73 us
  transfers between devices with their start and end apart: 2, of which 2 were waited for; matrix products, arithmetic and copies ran while one was open for 2% of the time, Pallas kernels for 0%

commit v1 on v0

--- a/solution.py
+++ b/solution.py
@@ -47,7 +47,10 @@
 
 
 def move_cols(tile):
-    return lax.all_to_all(tile, "col", split_axis=0, concat_axis=2, tiled=True)
+    return jnp.concatenate(
+        lax.all_to_all(jnp.stack(jnp.split(tile, lax.axis_size("col"), axis=0)), "col", 0, 0),
+        axis=2,
+    )
 
 
 def on_device(

time: 235 us -> 236 us (level)
  no operation moved by 1% of the time
where the time goes in v1:
time: 236 us
  waiting for transfers between devices  89.9 us (38%)
  blocking collectives  88.4 us (37%)
  local copies, waits for them, and re-layouts  19.7 us (8%)
  matrix products  18.8 us (8%)
  between operations  13.7 us (6%)
  other arithmetic  5.18 us (2%)
    all_gather x1, waiting for transfers between devices, gather_right(): return lax.all_gather(right_part, 'row', axis=1, tiled=True)  46.2 us
    all_to_all x2, blocking collectives, move_cols(): lax.all_to_all(jnp.stack(jnp.split(tile, lax.axis_size('col'), axis=0)),...  44.8 us
    all_gather x1, waiting for transfers between devices, on_device(): lax.all_gather(left_piece, 'seq', axis=0, tiled=True)  43 us
    all_to_all x1, blocking collectives, on_device(): lax.all_to_all(section_one.reshape(run_len, rowseq_count, own_rows, chann...  28 us
    all_gather x1, blocking collectives, on_device(): lax.all_gather(right_piece, 'seq', axis=0, tiled=True)  15.7 us
    dot_general x8, matrix products, project_block(): lax.dot_general(left_mat, right_mat, (((0,), (0,)), ((), ())), preferred_...  10.5 us
    dot_general x8, matrix products, project_block(): jnp.dot(outer_prod, proj_weight, preferred_element_type=jnp.float32)  6.24 us
    while x32, local copies, waits for them, and re-layouts  4.73 us
  transfers between devices with their start and end apart: 2, of which 2 were waited for; matrix products, arithmetic and copies ran while one was open for 2% of the time, Pallas kernels for 0%

profile of v1, /device:TPU:1, one launch (start us, length us, event | category | flops | bytes accessed | tf_op | source)
XLA Modules:
  0.0 236.0 jit_solution(3697710945286846450)
XLA Ops:
  7.3 15.7 %all_gather.10 = bf16[512,2,128]{2,1,0:T(2,128)(2,1)S(1)} all-gather(bf16[128,2,128]{2,1,0:T(2,128)(2,1)} %param.19), channel_id=1, replica_groups=mesh['row'=16,'col'=8,'seq'=4] {'seq'}, dimensions={0}, use_global_device_ids=true | all-gather | bytes 327680 | tf_op jit(solution)/shard_map/all_gather | solution.py:77
  23.8 43.0 %all-gather.3.cloned.1.call-done = bf16[512,32,64]{0,2,1:T(8,128)(2,1)} async-done(((bf16[128,32,64]{0,2,1:T(8,128)(2,1)}), bf16[512,32,64]{0,2,1:T(8,128)(2,1)}) %all-gather.3.cloned.1.call-update) | async-done | bytes 2097168 | tf_op jit(solution)/shard_map/all_gather | solution.py:76
  66.7 1.7 fusion.84
  69.9 46.2 %all-gather.5.cloned.1.call-done = bf16[512,32,128]{2,0,1:T(8,128)(2,1)} async-done(((bf16[512,2,128]{2,0,1:T(8,128)(2,1)}), bf16[512,32,128]{2,0,1:T(8,128)(2,1)}) %all-gather.5.cloned.1.call-update) | async-done | bytes 4194320 | tf_op jit(solution)/shard_map/all_gather | solution.py:46
  116.0 2.8 %fusion.83 = (bf16[128,32,128]{2,0,1:T(8,128)(2,1)S(1)}, bf16[128,32,128]{2,0,1:T(8,128)(2,1)S(1)}, bf16[128,32,128]{2,0,1:T(8,128)(2,1)S(1)}, bf16[128,32,128]{2,0,1:T(8,128)(2,1)S(1)}) fusion(bf16[512,32,128]{2,0,1:T(8,128)(2,1)} %all-gather.5.cloned.1.call-done), kind=kLoop, calls=%fused_computation.102 | loop fusion | bytes 8388608 | tf_op jit(solution)/shard_map/slice | solution.py:85
  120.9 1.7 copy.160
  122.6 1.1 broadcast.38.clone.2
  123.7 7.8 %while.40 = (s32[]{:T(128)}, f32[2,8,128,128]{3,2,1,0:T(8,128)}, bf16[2,128,32,8]{1,3,0,2:T(8,128)(2,1)}, bf16[128,32,128]{2,1,0:T(8,128)(2,1)}, bf16[1024,128]{1,0:T(8,128)(2,1)}, /*index=5*/s32[]{:T(128)}) while((s32[]{:T(128)}, f32[2,8,128,128]{3,2,1,0:T(8,128)}, bf16[2,128,32,8]{1,3,0,2:T(8,128)(2,1)}, bf16[128,32,128]{2,1,0:T(8,128)(2,1)}, ...), condition=%wide.region_1.2_spmd, body=%wide.region_0.1_spmd.sunk | while | flops 537919488 | bytes 15532201 | solution.py:28
  123.7 2.1 convolution_convert_fusion.8
  125.8 0.8 fusion.112
  126.6 1.0 copy-done.2
  127.6 2.1 convolution_convert_fusion.8
  129.7 0.8 fusion.112
  130.5 1.0 copy-done.2
  131.5 1.1 broadcast.38.clone.1
  132.5 6.9 %while.42 = (s32[]{:T(128)}, f32[2,8,128,128]{3,2,1,0:T(8,128)}, bf16[2,128,32,8]{1,3,0,2:T(8,128)(2,1)}, bf16[128,32,128]{2,1,0:T(8,128)(2,1)S(1)}, bf16[1024,128]{1,0:T(8,128)(2,1)}, /*index=5*/s32[]{:T(128)}) while((s32[]{:T(128)}, f32[2,8,128,128]{3,2,1,0:T(8,128)}, bf16[2,128,32,8]{1,3,0,2:T(8,128)(2,1)}, ...), condition=%wide.region_5.6_spmd, body=%wide.region_4.5_spmd.sunk | while | flops 537919488 | bytes 15532201 | solution.py:28
  132.5 1.7 convolution_convert_fusion.10
  134.2 0.8 fusion.122
  135.0 1.0 copy-done.5
  136.0 1.7 convolution_convert_fusion.10
  137.7 0.8 fusion.122
  138.5 1.0 copy-done.5
  139.6 3.5 %while.43 = (s32[]{:T(128)}, f32[2,8,128,128]{3,2,1,0:T(8,128)S(1)}, bf16[2,128,32,8]{1,3,0,2:T(8,128)(2,1)S(1)}, bf16[128,32,128]{2,1,0:T(8,128)(2,1)S(1)}, bf16[1024,128]{1,0:T(8,128)(2,1)}, /*index=5*/s32[]{:T(128)}) while((s32[]{:T(128)}, f32[2,8,128,128]{3,2,1,0:T(8,128)S(1)}, bf16[2,128,32,8]{1,3,0,2:T(8,128)(2,1)S(1)}, ...), condition=%wide.region_7.8_spmd, body=%wide.region_6.7_spmd.sunk | while | flops 537919488 | bytes 7143537 | solution.py:28
  143.2 0.9 copy-done.6
  144.1 3.6 %while.41 = (s32[]{:T(128)}, f32[2,8,128,128]{3,2,1,0:T(8,128)S(1)}, bf16[2,128,32,8]{1,3,0,2:T(8,128)(2,1)S(1)}, bf16[128,32,128]{2,1,0:T(8,128)(2,1)S(1)}, bf16[1024,128]{1,0:T(8,128)(2,1)}, /*index=5*/s32[]{:T(128)}) while((s32[]{:T(128)}, f32[2,8,128,128]{3,2,1,0:T(8,128)S(1)}, bf16[2,128,32,8]{1,3,0,2:T(8,128)(2,1)S(1)}, ...), condition=%wide.region_3.4_spmd, body=%wide.region_2.3_spmd.sunk | while | flops 537919488 | bytes 7143537 | solution.py:28
  145.1 0.8 fusion.117
  147.7 1.8 add_multiply_fusion
  151.0 24.2 %all_to_all.25 = bf16[8,1,2,128,128]{4,3,2,1,0:T(8,128)(2,1)S(1)} all-to-all(bf16[8,1,2,128,128]{4,3,2,1,0:T(8,128)(2,1)S(1)} %copy.168), channel_id=1, replica_groups=mesh['row'=16,'col'=8,'seq'=4] {'col'}, dimensions={0} | all-to-all | bytes 1048576 | tf_op jit(solution)/shard_map/all_to_all | solution.py:51
  175.3 28.0 %all_to_all.26 = bf16[2,64,16,128]{3,2,0,1:T(8,128)(2,1)S(1)} all-to-all(bf16[2,64,16,128]{3,2,0,1:T(8,128)(2,1)S(1)} %copy.170), channel_id=1, replica_groups=mesh['row'=16,'col'=8,'seq'=4] {'row','seq'}, dimensions={1} | all-to-all | bytes 1048576 | tf_op jit(solution)/shard_map/all_to_all | solution.py:92
  203.4 20.5 %all_to_all.27 = bf16[8,1,8,1,2,16,128]{6,5,4,2,3,1,0:T(8,128)(2,1)S(1)} all-to-all(bf16[8,1,8,1,2,16,128]{6,5,4,2,3,1,0:T(8,128)(2,1)S(1)} %fusion.65), channel_id=1, replica_groups=mesh['row'=16,'col'=8,'seq'=4] {'col'}, dimensions={0} | all-to-all | bytes 1048576 | tf_op jit(solution)/shard_map/all_to_all | solution.py:51
  224.1 1.0 fusion.60
  227.1 2.0 fusion.57
  (94 shorter events, 15.0 us)
Async XLA Ops:
  6.5 220.6 %copy-start = (bf16[512,128]{1,0:T(8,128)(2,1)S(1)}, bf16[512,128]{1,0:T(8,128)(2,1)}, u32[]{:S(2)}) copy-start(bf16[512,128]{1,0:T(8,128)(2,1)} %param.26) | copy-start | bytes 393220
  6.5 60.2 %all-gather.3.cloned.1.call-start = ((), (), s32[]{:S(2)}) async-start(), calls=%async_computation.3 | async-start | bytes 2621440 | tf_op jit(solution)/shard_map/all_gather | solution.py:76
  7.3 108.8 %all-gather.5.cloned.1.call-start = ((), (), s32[]{:S(2)}) async-start(), calls=%async_computation.4 | async-start | bytes 4456448 | tf_op jit(solution)/shard_map/all_gather | solution.py:46
  123.7 2.1 copy-start.1
  123.7 2.1 copy-start.10
  126.6 1.0 copy-start.2
  127.6 2.1 copy-start.1
  127.6 2.1 copy-start.10
  130.5 1.0 copy-start.2
  132.5 1.7 copy-start.4
  132.5 1.7 copy-start.11
  135.0 1.0 copy-start.5
  136.0 1.7 copy-start.4
  136.0 1.7 copy-start.11
  138.5 1.0 copy-start.5
  139.6 1.0 copy-start.12
  141.3 1.0 copy-start.12
  143.1 1.0 copy-start.6
  144.1 3.6 %copy-start.3 = (f32[2,8,128,128]{3,2,1,0:T(8,128)S(1)}, f32[2,8,128,128]{3,2,1,0:T(8,128)}, u32[]{:S(2)}) copy-start(f32[2,8,128,128]{3,2,1,0:T(8,128)} %get-tuple-element.113) | copy-start | bytes 3145732
  144.1 1.0 copy-start.13
  145.9 1.0 copy-start.13
  147.7 1.9 copy-start.8
  203.2 20.8 %copy-start.7 = (bf16[16,128,128]{2,1,0:T(8,128)(2,1)S(1)}, bf16[16,128,128]{2,1,0:T(8,128)(2,1)}, u32[]{:S(2)}) copy-start(bf16[16,128,128]{2,1,0:T(8,128)(2,1)} %param.22) | copy-start | bytes 1572868
  225.1 1.4 copy-start.9
  225.4 1.7 copy-start.14
  225.4 1.7 copy-start.15
  225.5 1.7 copy-start.16
Sparse Core Ops, SparseCore 0:
  9.4 57.2 all-gather.2
  68.9 47.1 all-gather.4
